TPU v7x, 32 devices: a whole 2x2x4 slice. The times are simulated.
32 devices in a mesh: dp: 8 (over z, x), seq: 4 (over y, core).
Axes of the slice: x: 2, y: 2, z: 4, core: 2. Of those that a mesh axis runs over, the one named last changes fastest.
Arguments:
- layer_input: bfloat16 [20480, 768], P(('dp', 'seq')), may hold values from -6 to 6
- segment_ids: int32 [8, 2560], P('dp'), may hold values from 0 to 2, never falling along the last dimension, each value on 1 to 2048 neighbouring positions
- cotangent: bfloat16 [20480, 768], P(('dp', 'seq')), may hold values from -6 to 6
- attn_gain: bfloat16 [768], replicated, may hold values from 0.25 to 1.75
- attn_shift: bfloat16 [768], replicated, may hold values from -1.796875 to 1.796875
- query_weight: bfloat16 [768, 768], P(None, 'seq'), may hold values from -0.21875 to 0.21875
- query_bias: bfloat16 [768], P('seq'), may hold values from -1.796875 to 1.796875
- key_weight: bfloat16 [768, 768], P(None, 'seq'), may hold values from -0.21875 to 0.21875
- value_weight: bfloat16 [768, 768], P(None, 'seq'), may hold values from -0.21875 to 0.21875
- value_bias: bfloat16 [768], P('seq'), may hold values from -0.1796875 to 0.1796875
- out_weight: bfloat16 [768, 768], P('seq'), may hold values from -6 to 6
- out_bias: bfloat16 [768], replicated, may hold values from -1.796875 to 1.796875
- ffn_gain: bfloat16 [768], replicated, may hold values from 0.25 to 1.75
- ffn_shift: bfloat16 [768], replicated, may hold values from -1.796875 to 1.796875
- up_weight: bfloat16 [768, 3072], P(None, 'seq'), may hold values from -0.21875 to 0.21875
- up_bias: bfloat16 [3072], P('seq'), may hold values from -1.796875 to 1.796875
- down_weight: bfloat16 [3072, 768], P('seq'), may hold values from -0.109375 to 0.109375
- down_bias: bfloat16 [768], replicated, may hold values from -1.796875 to 1.796875
Outputs:
- layer_output: bfloat16 [20480, 768], P(('dp', 'seq'))
- input_grad: float32 [20480, 768], P(('dp', 'seq'))
- grad_attn_gain: float32 [768], replicated
- grad_attn_shift: float32 [768], replicated
- grad_query_weight: float32 [768, 768], P(None, 'seq')
- grad_query_bias: float32 [768], P('seq')
- grad_key_weight: float32 [768, 768], P(None, 'seq')
- grad_value_weight: float32 [768, 768], P(None, 'seq')
- grad_value_bias: float32 [768], P('seq')
- grad_out_weight: float32 [768, 768], P('seq')
- grad_out_bias: float32 [768], replicated
- grad_ffn_gain: float32 [768], replicated
- grad_ffn_shift: float32 [768], replicated
- grad_up_weight: float32 [768, 3072], P(None, 'seq')
- grad_up_bias: float32 [3072], P('seq')
- grad_down_weight: float32 [3072, 768], P('seq')
- grad_down_bias: float32 [768], replicated
Inputs may be any that keep to these rules, and one draw needn't show every extreme that they name: `segment_ids`: along a row the ids never fall; each of the 3 ids covers 1 to 2048 consecutive tokens, and some document has exactly 2048 tokens.
All inputs are finite; a program needn't handle non-finite values.
Results may differ from a plain program's by a relative error of at most 0.014.
Values may be sent and summed in bfloat16 or wider, within the bound.
A program may use at most 192 MiB of HBM per device.

v0:
```python
import jax
import jax.numpy as jnp
from jax import lax
from jax.sharding import PartitionSpec as P

HEAD = 64
BLOCK = 512


EPSILON = 1e-06


def layer_norm(values, gain_row, shift_row):
    average = jnp.mean(values, axis=-1, keepdims=True)
    centered = values - average
    variance = jnp.mean(centered * centered, axis=-1, keepdims=True)
    return centered * lax.rsqrt(variance + EPSILON) * gain_row + shift_row


def exact_gelu(values):
    return jax.nn.gelu(values, approximate=False)


def matmul(left_side, right_side):
    return jnp.dot(left_side, right_side, preferred_element_type=jnp.float32)


def contract_rows(left_side, right_side):
    return lax.dot_general(
        left_side, right_side, (((0,), (0,)), ((), ())), preferred_element_type=jnp.float32
    )


def outer_back(left_side, right_side):
    return lax.dot_general(
        left_side, right_side, (((1,), (1,)), ((), ())), preferred_element_type=jnp.float32
    )


def block_bounds(segments):
    firsts = segments[::BLOCK]
    last_ids = segments[BLOCK - 1 :: BLOCK]
    lower_rows = jnp.sum((segments[None, :] < firsts[:, None]).astype(jnp.int32), axis=1)
    upper_rows = jnp.sum((segments[None, :] <= last_ids[:, None]).astype(jnp.int32), axis=1)
    return (lower_rows // BLOCK, (upper_rows + BLOCK - 1) // BLOCK)


def key_slices(key_three, value_three, segments, key_block):
    key_start = key_block * BLOCK
    return (
        key_start,
        lax.dynamic_slice_in_dim(key_three, key_start, BLOCK, 0),
        lax.dynamic_slice_in_dim(value_three, key_start, BLOCK, 0),
        lax.dynamic_slice_in_dim(segments, key_start, BLOCK, 0),
    )


def tile_probs(query_block, key_tile, seg_query, seg_key, log_total, score_scale):
    raw_scores = jnp.einsum(
        "qhd,khd->hqk", query_block, key_tile, preferred_element_type=jnp.float32
    )
    same_doc = (seg_query[:, None] == seg_key[None, :])[None]
    return jnp.where(same_doc, jnp.exp(raw_scores * score_scale - log_total[:, :, None]), 0.0)


def attend_forward(queries, key_rows, value_rows, segments, lower_tiles, upper_tiles, score_scale):
    length, row_width = queries.shape
    head_count = row_width // HEAD
    three_way = (length, head_count, HEAD)
    query_three = queries.reshape(three_way)
    key_three = key_rows.reshape(three_way)
    value_three = value_rows.reshape(three_way)

    def one_block(block_index):
        row_start = block_index * BLOCK
        query_block = lax.dynamic_slice_in_dim(query_three, row_start, BLOCK, 0)
        seg_query = lax.dynamic_slice_in_dim(segments, row_start, BLOCK, 0)

        def first_pass(key_block, carried):
            running, total_sum = carried
            unused_start, key_tile, unused_values, seg_key = key_slices(
                key_three, value_three, segments, key_block
            )
            raw_scores = jnp.einsum(
                "qhd,khd->hqk", query_block, key_tile, preferred_element_type=jnp.float32
            )
            same_doc = (seg_query[:, None] == seg_key[None, :])[None]
            scaled = jnp.where(same_doc, raw_scores * score_scale, -1e30)
            new_top = jnp.maximum(running, jnp.max(scaled, axis=-1))
            weights = jnp.where(same_doc, jnp.exp(scaled - new_top[:, :, None]), 0.0)
            return (new_top, total_sum * jnp.exp(running - new_top) + jnp.sum(weights, axis=-1))

        start_top = jnp.full((head_count, BLOCK), -1e30, jnp.float32)
        running, total_sum = lax.fori_loop(
            lower_tiles[block_index],
            upper_tiles[block_index],
            first_pass,
            (start_top, jnp.zeros((head_count, BLOCK), jnp.float32)),
        )
        log_total = running + jnp.log(total_sum)

        def second_pass(key_block, accumulated):
            unused_start, key_tile, value_tile, seg_key = key_slices(
                key_three, value_three, segments, key_block
            )
            weights_low = tile_probs(
                query_block, key_tile, seg_query, seg_key, log_total, score_scale
            ).astype(jnp.bfloat16)
            return accumulated + jnp.einsum(
                "hqk,khd->qhd", weights_low, value_tile, preferred_element_type=jnp.float32
            )

        mixed_rows = lax.fori_loop(
            lower_tiles[block_index],
            upper_tiles[block_index],
            second_pass,
            jnp.zeros((BLOCK, head_count, HEAD), jnp.float32),
        )
        return (mixed_rows.reshape(BLOCK, row_width), log_total)

    mixed_rows, log_totals = lax.map(one_block, jnp.arange(length // BLOCK, dtype=jnp.int32))
    return (mixed_rows.reshape(length, row_width), log_totals)


def attend_backward(
    queries,
    key_rows,
    value_rows,
    grad_mixed,
    segments,
    log_totals,
    lower_tiles,
    upper_tiles,
    score_scale,
):
    length, row_width = queries.shape
    head_count = row_width // HEAD
    three_way = (length, head_count, HEAD)
    query_three = queries.reshape(three_way)
    key_three = key_rows.reshape(three_way)
    value_three = value_rows.reshape(three_way)
    grad_three = grad_mixed.reshape(three_way)

    def one_block(block_index, carried):
        grad_keys, grad_values, grad_queries = carried
        row_start = block_index * BLOCK
        query_block = lax.dynamic_slice_in_dim(query_three, row_start, BLOCK, 0)
        grad_block = lax.dynamic_slice_in_dim(grad_three, row_start, BLOCK, 0)
        seg_query = lax.dynamic_slice_in_dim(segments, row_start, BLOCK, 0)
        log_total = log_totals[block_index]

        def tile_parts(key_block):
            key_start, key_tile, value_tile, seg_key = key_slices(
                key_three, value_three, segments, key_block
            )
            weights = tile_probs(query_block, key_tile, seg_query, seg_key, log_total, score_scale)
            grad_weights = jnp.einsum(
                "qhd,khd->hqk", grad_block, value_tile, preferred_element_type=jnp.float32
            )
            return (key_start, key_tile, weights, grad_weights)

        def delta_pass(key_block, delta_sum):
            unused_start, unused_tile, weights, grad_weights = tile_parts(key_block)
            return delta_sum + jnp.sum(weights * grad_weights, axis=-1)

        delta_sum = lax.fori_loop(
            lower_tiles[block_index],
            upper_tiles[block_index],
            delta_pass,
            jnp.zeros((head_count, BLOCK), jnp.float32),
        )

        def grad_pass(key_block, inner_carry):
            grad_query_block, grad_keys, grad_values = inner_carry
            key_start, key_tile, weights, grad_weights = tile_parts(key_block)
            grad_raw = (weights * (grad_weights - delta_sum[:, :, None]) * score_scale).astype(
                jnp.bfloat16
            )
            grad_query_block = grad_query_block + jnp.einsum(
                "hqk,khd->qhd", grad_raw, key_tile, preferred_element_type=jnp.float32
            )
            key_part = jnp.einsum(
                "hqk,qhd->khd", grad_raw, query_block, preferred_element_type=jnp.float32
            )
            value_part = jnp.einsum(
                "hqk,qhd->khd",
                weights.astype(jnp.bfloat16),
                grad_block,
                preferred_element_type=jnp.float32,
            )
            grad_keys = lax.dynamic_update_slice_in_dim(
                grad_keys,
                lax.dynamic_slice_in_dim(grad_keys, key_start, BLOCK, 0) + key_part,
                key_start,
                0,
            )
            grad_values = lax.dynamic_update_slice_in_dim(
                grad_values,
                lax.dynamic_slice_in_dim(grad_values, key_start, BLOCK, 0) + value_part,
                key_start,
                0,
            )
            return (grad_query_block, grad_keys, grad_values)

        grad_query_block, grad_keys, grad_values = lax.fori_loop(
            lower_tiles[block_index],
            upper_tiles[block_index],
            grad_pass,
            (jnp.zeros((BLOCK, head_count, HEAD), jnp.float32), grad_keys, grad_values),
        )
        grad_queries = lax.dynamic_update_slice_in_dim(grad_queries, grad_query_block, row_start, 0)
        return (grad_keys, grad_values, grad_queries)

    zero_three = jnp.zeros(three_way, jnp.float32)
    grad_keys, grad_values, grad_queries = lax.fori_loop(
        0, length // BLOCK, one_block, (zero_three, zero_three, zero_three)
    )
    return (
        grad_queries.reshape(length, row_width),
        grad_keys.reshape(length, row_width),
        grad_values.reshape(length, row_width),
    )


def local(
    layer_input,
    segment_ids,
    cotangent,
    attn_gain,
    attn_shift,
    query_weight,
    query_bias,
    key_weight,
    value_weight,
    value_bias,
    out_weight,
    out_bias,
    ffn_gain,
    ffn_shift,
    up_weight,
    up_bias,
    down_weight,
    down_bias,
):
    low_type = jnp.bfloat16
    score_scale = HEAD ** (-0.5)
    segments = segment_ids[0]
    lower_tiles, upper_tiles = block_bounds(segments)
    inputs = layer_input.astype(jnp.float32)
    normed_one, norm_one_back = jax.vjp(
        layer_norm, inputs, attn_gain.astype(jnp.float32), attn_shift.astype(jnp.float32)
    )
    normed_low = normed_one.astype(low_type)
    normed_rows = lax.all_gather(normed_low, "seq", axis=0, tiled=True)
    queries = (matmul(normed_rows, query_weight) + query_bias).astype(low_type)
    key_rows = matmul(normed_rows, key_weight).astype(low_type)
    value_rows = (matmul(normed_rows, value_weight) + value_bias).astype(low_type)
    mixed_float, log_totals = attend_forward(
        queries, key_rows, value_rows, segments, lower_tiles, upper_tiles, score_scale
    )
    mixed_low = mixed_float.astype(low_type)
    middle = inputs + (
        lax.psum_scatter(matmul(mixed_low, out_weight), "seq", scatter_dimension=0, tiled=True)
        + out_bias
    )
    normed_two, norm_two_back = jax.vjp(
        layer_norm, middle, ffn_gain.astype(jnp.float32), ffn_shift.astype(jnp.float32)
    )
    normed_rows_two, cotangent_rows = (
        lax.all_gather(normed_two.astype(low_type), "seq", axis=0, tiled=True),
        lax.all_gather(cotangent, "seq", axis=0, tiled=True),
    )
    pre_act = matmul(normed_rows_two, up_weight) + up_bias
    hidden_float, gelu_back = jax.vjp(exact_gelu, pre_act)
    hidden_low = hidden_float.astype(low_type)
    layer_output = (
        middle
        + lax.psum_scatter(
            matmul(hidden_low, down_weight).astype(jnp.bfloat16),
            "seq",
            scatter_dimension=0,
            tiled=True,
        ).astype(jnp.float32)
        + down_bias
    ).astype(low_type)
    grad_output = cotangent.astype(jnp.float32)
    grad_down_weight = contract_rows(hidden_low, cotangent_rows)
    grad_down_bias = jnp.sum(grad_output, axis=0)
    grad_pre = gelu_back(outer_back(cotangent_rows, down_weight))[0].astype(low_type)
    grad_up_bias = jnp.sum(grad_pre.astype(jnp.float32), axis=0)
    grad_up_weight = contract_rows(normed_rows_two, grad_pre)
    grad_normed_two = lax.psum_scatter(
        outer_back(grad_pre, up_weight), "seq", scatter_dimension=0, tiled=True
    )
    grad_mid_part, grad_ffn_gain, grad_ffn_shift = norm_two_back(grad_normed_two)
    grad_middle = grad_output + grad_mid_part
    grad_branch = grad_middle.astype(low_type)
    grad_out_bias = jnp.sum(grad_branch.astype(jnp.float32), axis=0)
    branch_rows = lax.all_gather(grad_branch, "seq", axis=0, tiled=True)
    grad_out_weight = contract_rows(mixed_low, branch_rows)
    grad_mixed = outer_back(branch_rows, out_weight).astype(low_type)
    grad_q_float, grad_k_float, grad_v_float = attend_backward(
        queries,
        key_rows,
        value_rows,
        grad_mixed,
        segments,
        log_totals,
        lower_tiles,
        upper_tiles,
        score_scale,
    )
    grad_q_low = grad_q_float.astype(low_type)
    grad_k_low = grad_k_float.astype(low_type)
    grad_v_low = grad_v_float.astype(low_type)
    grad_query_weight = contract_rows(normed_rows, grad_q_low)
    grad_key_weight = contract_rows(normed_rows, grad_k_low)
    grad_value_weight = contract_rows(normed_rows, grad_v_low)
    grad_query_bias = jnp.sum(grad_q_low.astype(jnp.float32), axis=0)
    grad_value_bias = jnp.sum(grad_v_low.astype(jnp.float32), axis=0)
    part_q = outer_back(grad_q_low, query_weight)
    part_k = outer_back(grad_k_low, key_weight)
    part_v = outer_back(grad_v_low, value_weight)
    grad_normed_one = lax.psum_scatter(
        (part_q + part_k + part_v).astype(jnp.bfloat16), "seq", scatter_dimension=0, tiled=True
    ).astype(jnp.float32)
    grad_in_part, grad_attn_gain, grad_attn_shift = norm_one_back(grad_normed_one)
    input_grad = grad_middle + grad_in_part
    (
        grad_query_weight,
        grad_key_weight,
        grad_value_weight,
        grad_out_weight,
        grad_up_weight,
        grad_down_weight,
        grad_query_bias,
        grad_value_bias,
        grad_up_bias,
    ) = lax.psum(
        (
            grad_query_weight,
            grad_key_weight,
            grad_value_weight,
            grad_out_weight,
            grad_up_weight,
            grad_down_weight,
            grad_query_bias,
            grad_value_bias,
            grad_up_bias,
        ),
        "dp",
    )
    (
        grad_attn_gain,
        grad_attn_shift,
        grad_out_bias,
        grad_ffn_gain,
        grad_ffn_shift,
        grad_down_bias,
    ) = lax.psum(
        (
            grad_attn_gain,
            grad_attn_shift,
            grad_out_bias,
            grad_ffn_gain,
            grad_ffn_shift,
            grad_down_bias,
        ),
        ("dp", "seq"),
    )
    return (
        layer_output,
        input_grad,
        grad_attn_gain,
        grad_attn_shift,
        grad_query_weight,
        grad_query_bias,
        grad_key_weight,
        grad_value_weight,
        grad_value_bias,
        grad_out_weight,
        grad_out_bias,
        grad_ffn_gain,
        grad_ffn_shift,
        grad_up_weight,
        grad_up_bias,
        grad_down_weight,
        grad_down_bias,
    )


def solution(mesh):
    return jax.shard_map(
        local,
        mesh=mesh,
        in_specs=(
            P(("dp", "seq"), None),
            P("dp", None),
            P(("dp", "seq"), None),
            P(),
            P(),
            P(None, "seq"),
            P("seq"),
            P(None, "seq"),
            P(None, "seq"),
            P("seq"),
            P("seq", None),
            P(),
            P(),
            P(),
            P(None, "seq"),
            P("seq"),
            P("seq", None),
            P(),
        ),
        out_specs=(
            P(("dp", "seq"), None),
            P(("dp", "seq"), None),
            P(),
            P(),
            P(None, "seq"),
            P("seq"),
            P(None, "seq"),
            P(None, "seq"),
            P("seq"),
            P("seq", None),
            P(),
            P(),
            P(),
            P(None, "seq"),
            P("seq"),
            P("seq", None),
            P(),
        ),
        check_vma=False,
    )
```

profile of v0, /device:TPU:0, one launch (start us, length us, event | category | flops | bytes accessed | tf_op | source)
XLA Modules:
  0.0 1368.7 jit_solution(13079674862722004424)
XLA Ops:
  15.6 35.2 %all-gather.5.cloned.1.call-done = bf16[2560,768]{1,0:T(8,128)(2,1)} async-done(((bf16[640,768]{1,0:T(8,128)(2,1)}), bf16[2560,768]{1,0:T(8,128)(2,1)}) %all-gather.5.cloned.1.call-update) | async-done | bytes 3932176 | tf_op jit(solution)/shard_map/all_gather | solution.py:254
  59.4 181.3 %while.105 = (s32[]{:T(128)}, bf16[5,512,192]{1,2,0:T(8,128)(2,1)}, f32[5,3,512]{2,1,0:T(4,128)S(1)}, s32[5]{0:T(128)S(1)}, s32[5]{0:T(128)S(1)}, /*index=5*/s32...) while((s32[]{:T(128)}, bf16[5,512,192]{1,2,0:T(8,128)(2,1)}, ...), condition=%wide.region_11.12_spmd, body=%wide.region_4.11_spmd.sunk | while | flops 312054272 | bytes 11100563 | solution.py:121
  65.4 11.0 while.109
  76.5 23.3 %while.110 = (s32[]{:T(128)}, f32[512,3,64]{0,2,1:T(8,128)S(1)}, s32[]{:T(128)}, bf16[2560,3,64]{0,2,1:T(8,128)(2,1)}, s32[512]{0:T(512)S(1)}, /*index=5*/s32[25...) while((s32[]{:T(128)}, f32[512,3,64]{0,2,1:T(8,128)S(1)}, ...), condition=%wide.region_10.10_spmd, body=%wide.region_9.9_spmd.sunk | while | flops 204832768 | bytes 1918127 | solution.py:113
  106.5 11.0 while.109
  117.6 23.3 %while.110 = (s32[]{:T(128)}, f32[512,3,64]{0,2,1:T(8,128)S(1)}, s32[]{:T(128)}, bf16[2560,3,64]{0,2,1:T(8,128)(2,1)}, s32[512]{0:T(512)S(1)}, /*index=5*/s32[25...) while((s32[]{:T(128)}, f32[512,3,64]{0,2,1:T(8,128)S(1)}, ...), condition=%wide.region_10.10_spmd, body=%wide.region_9.9_spmd.sunk | while | flops 204832768 | bytes 1918127 | solution.py:113
  147.6 11.0 while.109
  158.7 23.3 %while.110 = (s32[]{:T(128)}, f32[512,3,64]{0,2,1:T(8,128)S(1)}, s32[]{:T(128)}, bf16[2560,3,64]{0,2,1:T(8,128)(2,1)}, s32[512]{0:T(512)S(1)}, /*index=5*/s32[25...) while((s32[]{:T(128)}, f32[512,3,64]{0,2,1:T(8,128)S(1)}, ...), condition=%wide.region_10.10_spmd, body=%wide.region_9.9_spmd.sunk | while | flops 204832768 | bytes 1918127 | solution.py:113
  188.7 11.0 while.109
  199.8 23.3 %while.110 = (s32[]{:T(128)}, f32[512,3,64]{0,2,1:T(8,128)S(1)}, s32[]{:T(128)}, bf16[2560,3,64]{0,2,1:T(8,128)(2,1)}, s32[512]{0:T(512)S(1)}, /*index=5*/s32[25...) while((s32[]{:T(128)}, f32[512,3,64]{0,2,1:T(8,128)S(1)}, ...), condition=%wide.region_10.10_spmd, body=%wide.region_9.9_spmd.sunk | while | flops 204832768 | bytes 1918127 | solution.py:113
  248.3 133.1 %reduce-scatter.5.cloned.1.call-done = f32[640,768]{1,0:T(8,128)} async-done(((f32[2560,768]{1,0:T(8,128)}), f32[640,768]{1,0:T(8,128)}) %reduce-scatter.5.cloned.1.call-update) | async-done | bytes 1966096 | tf_op jit(solution)/shard_map/reduce_scatter | solution.py:263
  386.7 32.3 %all-gather.7.cloned.1.call-done = bf16[2560,768]{1,0:T(8,128)(2,1)} async-done(((bf16[640,768]{1,0:T(8,128)(2,1)}), bf16[2560,768]{1,0:T(8,128)(2,1)}) %all-gather.7.cloned.1.call-update) | async-done | bytes 3932176 | tf_op jit(solution)/shard_map/all_gather | solution.py:270
  419.1 8.9 fusion.76
  428.0 25.6 %all-gather.9.cloned.1.call-done = bf16[2560,768]{1,0:T(8,128)(2,1)} async-done(((bf16[640,768]{1,0:T(8,128)(2,1)}), bf16[2560,768]{1,0:T(8,128)(2,1)}) %all-gather.9.cloned.1.call-update) | async-done | bytes 3932176 | tf_op jit(solution)/shard_map/all_gather | solution.py:271
  453.6 24.4 %convert_reduce_fusion = (f32[768]{0:T(1024)}, bf16[2560,768]{1,0:T(8,128)(2,1)S(1)}, f32[2560,768]{1,0:T(8,128)}) fusion(f32[2560,768]{1,0:T(8,128)} %fusion.76, f32[768]{0:T(1024)S(1)} %convert_element_type.147, bf16[2560,768]{1,0:T(8,128)(2,1)} %all-gather.9.cloned.1.call-done, bf16[768,768]{1,0:T(8,128)(2,1)S(1)} %copy-done), kind=kOutput, calls=%fused_computation.63 | convolution fusion | flops 3167354112 | bytes 24778752 | tf_op jit(solution)/shard_map/dot_general | solution.py:35
  499.2 55.1 %reduce-scatter.9.cloned.1.call-done = f32[640,768]{1,0:T(8,128)} async-done(((f32[2560,768]{1,0:T(8,128)}), f32[640,768]{1,0:T(8,128)}) %reduce-scatter.9.cloned.1.call-update) | async-done | bytes 1966096 | tf_op jit(solution)/shard_map/reduce_scatter | solution.py:292
  557.8 41.8 %reduce-scatter.7.cloned.1.call-done = bf16[640,768]{1,0:T(8,128)(2,1)} async-done(((bf16[2560,768]{1,0:T(8,128)(2,1)}), bf16[640,768]{1,0:T(8,128)(2,1)}) %reduce-scatter.7.cloned.1.call-update) | async-done | bytes 983056 | tf_op jit(solution)/shard_map/reduce_scatter | solution.py:278
  607.3 33.0 %all-gather.11.cloned.1.call-done = bf16[2560,768]{1,0:T(8,128)(2,1)} async-done(((bf16[640,768]{1,0:T(8,128)(2,1)}), bf16[2560,768]{1,0:T(8,128)(2,1)}) %all-gather.11.cloned.1.call-update) | async-done | bytes 3932176 | tf_op jit(solution)/shard_map/all_gather | solution.py:299
  647.8 286.1 %while.108 = (s32[]{:T(128)}, f32[2560,3,64]{0,2,1:T(8,128)}, f32[2560,3,64]{0,2,1:T(8,128)}, bf16[2560,3,64]{0,2,1:T(8,128)(2,1)S(1)}, s32[5]{0:T(128)S(1)}, /*...) while((s32[]{:T(128)}, f32[2560,3,64]{0,2,1:T(8,128)}, ...), condition=%wide.region_25.26_spmd, body=%wide.region_19.25_spmd.sunk | while | flops 718045184 | bytes 28335068 | solution.py:215
  650.8 15.7 %while.111 = (s32[]{:T(128)}, f32[3,512]{1,0:T(4,128)S(1)}, s32[]{:T(128)}, s32[512]{0:T(512)S(1)}, s32[2560]{0:T(1024)S(1)}, /*index=5*/bf16[2560,3,64]{0,2,1:T...) while((s32[]{:T(128)}, f32[3,512]{1,0:T(4,128)S(1)}, ...), condition=%wide.region_22.22_spmd, body=%wide.region_20.21_spmd.sunk | while | flops 205520896 | bytes 7641279 | solution.py:166
  666.5 47.6 %while.112 = (s32[]{:T(128)}, f32[512,3,64]{0,2,1:T(8,128)S(1)}, f32[2560,3,64]{0,2,1:T(8,128)}, f32[2560,3,64]{0,2,1:T(8,128)}, s32[]{:T(128)}, /*index=5*/bf16...) while((s32[]{:T(128)}, f32[512,3,64]{0,2,1:T(8,128)S(1)}, ...), condition=%wide.region_24.24_spmd, body=%wide.region_23.23_spmd.sunk | while | flops 512524288 | bytes 18704612 | solution.py:205
  717.2 15.7 %while.111 = (s32[]{:T(128)}, f32[3,512]{1,0:T(4,128)S(1)}, s32[]{:T(128)}, s32[512]{0:T(512)S(1)}, s32[2560]{0:T(1024)S(1)}, /*index=5*/bf16[2560,3,64]{0,2,1:T...) while((s32[]{:T(128)}, f32[3,512]{1,0:T(4,128)S(1)}, ...), condition=%wide.region_22.22_spmd, body=%wide.region_20.21_spmd.sunk | while | flops 205520896 | bytes 7641279 | solution.py:166
  732.9 47.6 %while.112 = (s32[]{:T(128)}, f32[512,3,64]{0,2,1:T(8,128)S(1)}, f32[2560,3,64]{0,2,1:T(8,128)}, f32[2560,3,64]{0,2,1:T(8,128)}, s32[]{:T(128)}, /*index=5*/bf16...) while((s32[]{:T(128)}, f32[512,3,64]{0,2,1:T(8,128)S(1)}, ...), condition=%wide.region_24.24_spmd, body=%wide.region_23.23_spmd.sunk | while | flops 512524288 | bytes 18704612 | solution.py:205
  783.6 15.7 %while.111 = (s32[]{:T(128)}, f32[3,512]{1,0:T(4,128)S(1)}, s32[]{:T(128)}, s32[512]{0:T(512)S(1)}, s32[2560]{0:T(1024)S(1)}, /*index=5*/bf16[2560,3,64]{0,2,1:T...) while((s32[]{:T(128)}, f32[3,512]{1,0:T(4,128)S(1)}, ...), condition=%wide.region_22.22_spmd, body=%wide.region_20.21_spmd.sunk | while | flops 205520896 | bytes 7641279 | solution.py:166
  799.4 47.6 %while.112 = (s32[]{:T(128)}, f32[512,3,64]{0,2,1:T(8,128)S(1)}, f32[2560,3,64]{0,2,1:T(8,128)}, f32[2560,3,64]{0,2,1:T(8,128)}, s32[]{:T(128)}, /*index=5*/bf16...) while((s32[]{:T(128)}, f32[512,3,64]{0,2,1:T(8,128)S(1)}, ...), condition=%wide.region_24.24_spmd, body=%wide.region_23.23_spmd.sunk | while | flops 512524288 | bytes 18704612 | solution.py:205
  850.1 15.7 %while.111 = (s32[]{:T(128)}, f32[3,512]{1,0:T(4,128)S(1)}, s32[]{:T(128)}, s32[512]{0:T(512)S(1)}, s32[2560]{0:T(1024)S(1)}, /*index=5*/bf16[2560,3,64]{0,2,1:T...) while((s32[]{:T(128)}, f32[3,512]{1,0:T(4,128)S(1)}, ...), condition=%wide.region_22.22_spmd, body=%wide.region_20.21_spmd.sunk | while | flops 205520896 | bytes 7641279 | solution.py:166
  865.8 47.6 %while.112 = (s32[]{:T(128)}, f32[512,3,64]{0,2,1:T(8,128)S(1)}, f32[2560,3,64]{0,2,1:T(8,128)}, f32[2560,3,64]{0,2,1:T(8,128)}, s32[]{:T(128)}, /*index=5*/bf16...) while((s32[]{:T(128)}, f32[512,3,64]{0,2,1:T(8,128)S(1)}, ...), condition=%wide.region_24.24_spmd, body=%wide.region_23.23_spmd.sunk | while | flops 512524288 | bytes 18704612 | solution.py:205
  921.0 12.9 while.112
  942.3 8.1 fusion.81
  964.0 145.6 %all-reduce.1 = (f32[192]{0:T(256)}, f32[192]{0:T(256)}, f32[768]{0:T(1024)}) all-reduce(f32[192]{0:T(256)S(1)} %reduce_sum.238, f32[192]{0:T(256)S(1)} %reduce_sum.240, f32[768]{0:T(1024)S(1)} %copy-done.43), channel_id=1, replica_groups=mesh['dp'=8,'seq'=4] {'dp'}, use_global_device_ids=true, to_apply=%region_35.36 | all-reduce | flops 1152 | bytes 9216 | tf_op jit(solution)/shard_map/psum | solution.py:339
  1116.3 41.4 %all-reduce = (f32[768]{0:T(1024)}, f32[768]{0:T(1024)}, f32[768]{0:T(1024)}, f32[768]{0:T(1024)}, f32[768]{0:T(1024)}, /*index=5*/f32[768]{0:T(1024)}) all-reduce(f32[768]{0:T(1024)S(1)} %get-tuple-element.533, f32[768]{0:T(1024)S(1)} %get-tuple-element.536, f32[768]{0:T(1024)S(1)} %copy-done.41, ...), channel_id=1, replica_groups=mesh['dp'=8,'seq'=4] {'dp','seq'}, use_global_device_ids=true, to_apply=%region_30.31 | all-reduce | flops 4608 | bytes 36864 | tf_op jit(solution)/shard_map/psum | solution.py:360
  1157.7 194.7 %all-reduce.5.cloned.1.call-done = (f32[768,192]{0,1:T(8,128)}, f32[768,192]{0,1:T(8,128)}, f32[768,192]{0,1:T(8,128)}, f32[192,768]{1,0:T(8,128)}, f32[768,768]{1,0:T(8,128)}, /*index=5*/f32[768,768]{1,0:T(8,128)}) async-done(((f32[768,192]{0,1:T(8,128)}, f32[768,192]{0,1:T(8,128)}, f32[768,192]{0,1:T(8,128)}, f32[192,768]{1,0:T(8,128)}, f32[768,768]{1,0:T(8,128)}, /*index=5*/f32[768,768]{1,0:T(8,128)}), ...) | async-done | bytes 7077904 | tf_op jit(solution)/shard_map/psum | solution.py:339
  (664 shorter events, 419.5 us)
Async XLA Ops:
  7.2 446.4 %copy-start = (bf16[768,768]{1,0:T(8,128)(2,1)S(1)}, bf16[768,768]{1,0:T(8,128)(2,1)}, u32[]{:S(2)}) copy-start(bf16[768,768]{1,0:T(8,128)(2,1)} %param.46) | copy-start | bytes 3538948
  7.2 7.8 copy-start.42
  7.2 8.1 copy-start.52
  7.2 8.1 copy-start.53
  7.2 43.6 %copy-start.23 = (bf16[768,192]{0,1:T(8,128)(2,1)S(1)}, bf16[768,192]{0,1:T(8,128)(2,1)}, u32[]{:S(2)}) copy-start(bf16[768,192]{0,1:T(8,128)(2,1)} %param.37) | copy-start | bytes 884740
  7.2 43.6 %all-gather.5.cloned.1.call-start = ((), (), s32[]{:S(2)}) async-start(), calls=%async_computation.4 | async-start | bytes 4915200 | tf_op jit(solution)/shard_map/all_gather | solution.py:254
  8.8 6.8 copy-start.29
  15.0 366.4 %reduce-scatter.5.cloned.1.call-start = ((), (), s32[]{:S(2)}) async-start(), calls=%async_computation.5 | async-start | bytes 9830400 | tf_op jit(solution)/shard_map/reduce_scatter | solution.py:263
  15.6 38.9 %copy-start.25 = (bf16[768,192]{0,1:T(8,128)(2,1)S(1)}, bf16[768,192]{0,1:T(8,128)(2,1)}, u32[]{:S(2)}) copy-start(bf16[768,192]{0,1:T(8,128)(2,1)} %param.35) | copy-start | bytes 884740
  247.6 133.8 %copy-start.4 = (bf16[640,768]{1,0:T(8,128)(2,1)S(1)}, bf16[640,768]{1,0:T(8,128)(2,1)}, u32[]{:S(2)}) copy-start(bf16[640,768]{1,0:T(8,128)(2,1)} %param.30) | copy-start | bytes 2949124
  247.6 171.4 %all-gather.7.cloned.1.call-start = ((), (), s32[]{:S(2)}) async-start(), calls=%async_computation.6 | async-start | bytes 4915200 | tf_op jit(solution)/shard_map/all_gather | solution.py:270
  385.9 67.7 %all-gather.9.cloned.1.call-start = ((), (), s32[]{:S(2)}) async-start(), calls=%async_computation.8 | async-start | bytes 4915200 | tf_op jit(solution)/shard_map/all_gather | solution.py:271
  386.5 167.8 %reduce-scatter.9.cloned.1.call-start = ((), (), s32[]{:S(2)}) async-start(), calls=%async_computation.9 | async-start | bytes 9830400 | tf_op jit(solution)/shard_map/reduce_scatter | solution.py:292
  453.6 26.2 %copy-start.51 = (bf16[768,768]{1,0:T(8,128)(2,1)S(1)}, bf16[768,768]{1,0:T(8,128)(2,1)}, u32[]{:S(2)}) copy-start(bf16[768,768]{1,0:T(8,128)(2,1)} %param.44) | copy-start | bytes 3538948
  485.2 114.5 %reduce-scatter.7.cloned.1.call-start = ((), (), s32[]{:S(2)}) async-start(), calls=%async_computation.7 | async-start | bytes 4915200 | tf_op jit(solution)/shard_map/reduce_scatter | solution.py:278
  498.6 141.7 %all-gather.11.cloned.1.call-start = ((), (), s32[]{:S(2)}) async-start(), calls=%async_computation.10 | async-start | bytes 4915200 | tf_op jit(solution)/shard_map/all_gather | solution.py:299
  557.8 47.4 %copy-start.13 = (bf16[640,768]{1,0:T(8,128)(2,1)S(1)}, bf16[640,768]{1,0:T(8,128)(2,1)}, u32[]{:S(2)}) copy-start(bf16[640,768]{1,0:T(8,128)(2,1)} %param.32) | copy-start | bytes 2949124
  603.8 36.5 %copy-start.22 = (bf16[192,768]{1,0:T(8,128)(2,1)S(1)}, bf16[192,768]{1,0:T(8,128)(2,1)}, u32[]{:S(2)}) copy-start(bf16[192,768]{1,0:T(8,128)(2,1)} %param.40) | copy-start | bytes 884740
  603.8 41.0 %copy-start.37 = (f32[640]{0:T(1024)}, f32[640]{0:T(1024)S(1)}, u32[]{:S(2)}) copy-start(f32[640]{0:T(1024)S(1)} %negate_multiply_fusion.2) | copy-start | bytes 7684
  607.1 502.5 %reduce-scatter.11.cloned.1.call-start = ((), (), s32[]{:S(2)}) async-start(), calls=%async_computation.11 | async-start | bytes 4915200 | tf_op jit(solution)/shard_map/reduce_scatter | solution.py:324
  941.9 410.5 %all-reduce.5.cloned.1.call-start = ((), (), s32[]{:S(2)}) async-start(), calls=%async_computation.12 | async-start | bytes 14155776 | tf_op jit(solution)/shard_map/psum | solution.py:339
  942.3 8.2 copy-start.18
  942.3 8.2 copy-start.49
  963.3 146.3 %copy-start.5 = (bf16[640,768]{1,0:T(8,128)(2,1)S(1)}, bf16[640,768]{1,0:T(8,128)(2,1)}, u32[]{:S(2)}) copy-start(bf16[640,768]{1,0:T(8,128)(2,1)} %param.30) | copy-start | bytes 2949124
  963.3 146.3 %copy-start.30 = (f32[640]{0:T(1024)S(1)}, f32[640]{0:T(1024)}, u32[]{:S(2)}) copy-start(f32[640]{0:T(1024)} %copy-done.29) | copy-start | bytes 7684
  963.3 146.3 %copy-start.32 = (f32[768]{0:T(1024)S(1)}, f32[768]{0:T(1024)}, u32[]{:S(2)}) copy-start(f32[768]{0:T(1024)} %copy-done.31) | copy-start | bytes 9220
  963.3 148.4 %copy-start.36 = (f32[640]{0:T(1024)S(1)}, f32[640]{0:T(1024)}, u32[]{:S(2)}) copy-start(f32[640]{0:T(1024)} %copy-done.35) | copy-start | bytes 7684
  963.4 148.4 %copy-start.34 = (f32[640]{0:T(1024)S(1)}, f32[640]{0:T(1024)}, u32[]{:S(2)}) copy-start(f32[640]{0:T(1024)} %copy-done.33) | copy-start | bytes 7684
  963.4 150.7 %copy-start.14 = (bf16[640,768]{1,0:T(8,128)(2,1)S(1)}, bf16[640,768]{1,0:T(8,128)(2,1)}, u32[]{:S(2)}) copy-start(bf16[640,768]{1,0:T(8,128)(2,1)} %param.32) | copy-start | bytes 2949124
  963.4 150.7 %copy-start.38 = (f32[640]{0:T(1024)S(1)}, f32[640]{0:T(1024)}, u32[]{:S(2)}) copy-start(f32[640]{0:T(1024)} %copy-done.37) | copy-start | bytes 7684
  1352.4 5.9 copy-start.21
  1352.4 6.7 copy-start.20
  (32 other events, 73.5 us)
Sparse Core Ops, SparseCore 0:
  15.1 35.6 all-gather.4
  247.8 133.6 reduce-scatter.4
  386.0 32.9 all-gather.6
  420.6 32.9 all-gather.8
  485.3 68.9 reduce-scatter.8
  556.7 42.8 reduce-scatter.6
  607.3 32.9 all-gather.10
  942.0 165.7 reduce-scatter.10
  1113.9 238.4 all-reduce.4
where the time goes:
time: 1380 us; the launch traced here: 1370 us
  waiting for transfers between devices  552 us (40%)
  matrix products  321 us (23%)
  blocking collectives  187 us (14%)
  loops' own time  170 us (12%)
  other arithmetic  64.9 us (5%)
  local copies, waits for them, and re-layouts  58.6 us (4%)
  between operations  14.6 us (1%)
    psum x1, waiting for transfers between devices, local(): lax.psum((grad_query_weight, grad_key_weight, grad_value_weight, grad_out...  195 us
    psum x1, blocking collectives, local(): lax.psum((grad_query_weight, grad_key_weight, grad_value_weight, grad_out...  146 us
    reduce_scatter x1, waiting for transfers between devices, local(): lax.psum_scatter(matmul(mixed_low, out_weight), 'seq', scatter_dimension=...  133 us
    dot_general x34, matrix products, tile_parts(): jnp.einsum('qhd,khd->hqk', grad_block, value_tile, preferred_element_type...  74 us
    another operation x5, loops' own time, one_block(): lax.fori_loop(lower_tiles[block_index], upper_tiles[block_index], grad_pa...  59.8 us
    another operation x5, loops' own time, one_block(): lax.fori_loop(lower_tiles[block_index], upper_tiles[block_index], second_...  59.6 us
    reduce_scatter x1, waiting for transfers between devices, local(): lax.psum_scatter(outer_back(grad_pre, up_weight), 'seq', scatter_dimensio...  55.1 us
    dot_general x17, matrix products, grad_pass(): jnp.einsum('hqk,qhd->khd', weights.astype(jnp.bfloat16), grad_block, pref...  43.6 us
  transfers between devices with their start and end apart: 9, of which 8 were waited for; matrix products, arithmetic and copies ran while one was open for 4% of the time, Pallas kernels for 0%

commit v1 on v0

v1 whole, which is shorter than its diff:
```python
import functools

import jax
import jax.numpy as jnp
from jax import lax
from jax.experimental import pallas as pl
from jax.experimental.pallas import tpu as pltpu
from jax.sharding import PartitionSpec as P

HEAD = 64
SCALE = HEAD ** (-0.5)
LOG_SCALE = SCALE * 1.4426950408889634
LONGEST = 2048
NN = (((1,), (0,)), ((), ()))
NT = (((1,), (1,)), ((), ()))


EPSILON = 1e-06


def layer_norm(values, gain_row, shift_row):
    average = jnp.mean(values, axis=-1, keepdims=True)
    centered = values - average
    variance = jnp.mean(centered * centered, axis=-1, keepdims=True)
    return centered * lax.rsqrt(variance + EPSILON) * gain_row + shift_row


def exact_gelu(values):
    return jax.nn.gelu(values, approximate=False)


def matmul(left_side, right_side):
    return jnp.dot(left_side, right_side, preferred_element_type=jnp.float32)


def contract_rows(left_side, right_side):
    return lax.dot_general(
        left_side, right_side, (((0,), (0,)), ((), ())), preferred_element_type=jnp.float32
    )


def outer_back(left_side, right_side):
    return lax.dot_general(
        left_side, right_side, (((1,), (1,)), ((), ())), preferred_element_type=jnp.float32
    )


def rotation(segments, longest):
    zeros = jnp.sum((segments == 0).astype(jnp.int32))
    ones = jnp.sum((segments == 1).astype(jnp.int32))
    twos = segments.shape[0] - zeros - ones
    offset = jnp.where(zeros == longest, 0, jnp.where(ones == longest, zeros, zeros + ones))
    border = jnp.where(zeros == longest, ones, jnp.where(ones == longest, twos, zeros))
    return jnp.stack([offset, border])


def dot(left_side, right_side, dims):
    return lax.dot_general(left_side, right_side, dims, preferred_element_type=jnp.float32)


def keep_head(head, values):
    lane = lax.broadcasted_iota(jnp.int32, values.shape, 1)
    inside = (lane >= head * HEAD) & (lane < (head + 1) * HEAD)
    return jnp.where(inside, values, jnp.zeros_like(values))


def forward_kernel(
    rows_of, keys_of, head_count, spans, q_ref, k_ref, v_ref, mixed_ref, mixed_rot_ref, log_ref, q_rot, k_rot, v_heads
):
    length, width = q_ref.shape
    small = length - LONGEST
    offset, border = spans[0], spans[1]

    def rotated(ref):
        return pltpu.roll(ref[...].astype(jnp.float32), length - offset, 0).astype(jnp.bfloat16)

    q_rot[...] = rotated(q_ref)
    k_rot[...] = rotated(k_ref)
    v_all = rotated(v_ref)
    for head in range(head_count):
        v_heads[head] = jnp.concatenate(
            [keep_head(head, v_all), jnp.full((length, 256 - width), 1, jnp.bfloat16)], axis=1
        )

    def block(row, key_base, key_count, masked):
        rows = pl.ds(row, rows_of)
        total = jnp.zeros((rows_of, width), jnp.float32)
        logs = []
        for head in range(head_count):
            q_head = keep_head(head, q_rot[rows, :])
            top, parts = None, []
            for chunk in range(key_count // keys_of):
                keys = pl.ds(key_base + chunk * keys_of, keys_of)
                scores = dot(q_head, k_rot[keys, :], NT)
                if masked:
                    shape = (rows_of, keys_of)
                    row_id = lax.broadcasted_iota(jnp.int32, shape, 0) + (row - LONGEST)
                    key_id = lax.broadcasted_iota(jnp.int32, shape, 1) + chunk * keys_of
                    scores = jnp.where((row_id < border) == (key_id < border), scores, -1e30)
                high = jnp.max(scores, axis=1, keepdims=True)
                top = high if top is None else jnp.maximum(top, high)
                parts.append(scores)
            summed = jnp.zeros((rows_of, 256), jnp.float32)
            for chunk, scores in enumerate(parts):
                keys = pl.ds(key_base + chunk * keys_of, keys_of)
                weights = jnp.exp2((scores - top) * LOG_SCALE).astype(jnp.bfloat16)
                summed = summed + dot(weights, v_heads[head, keys, :], NN)
            norm = summed[:, 255:256]
            total = total + summed[:, :width] * (1.0 / norm)
            logs.append(top * LOG_SCALE + jnp.log2(norm))
        mixed_rot_ref[rows, :] = total
        logs.append(jnp.zeros((rows_of, 128 - head_count), jnp.float32))
        log_ref[rows, :] = jnp.concatenate(logs, axis=1)

    def large(index, nothing):
        block(pl.multiple_of(index * rows_of, rows_of), 0, LONGEST, False)
        return nothing

    def little(index, nothing):
        block(pl.multiple_of(LONGEST + index * rows_of, rows_of), LONGEST, small, True)
        return nothing

    lax.fori_loop(0, LONGEST // rows_of, large, 0)
    lax.fori_loop(0, small // rows_of, little, 0)
    mixed_ref[...] = pltpu.roll(mixed_rot_ref[...], offset, 0).astype(jnp.bfloat16)


def attend_forward(spans, queries, key_rows, value_rows):
    length, width = queries.shape
    head_count = width // HEAD
    vmem = pl.BlockSpec(memory_space=pltpu.VMEM)
    return pl.pallas_call(
        functools.partial(forward_kernel, 512, 512, head_count),
        out_shape=(
            jax.ShapeDtypeStruct((length, width), jnp.bfloat16),
            jax.ShapeDtypeStruct((length, width), jnp.float32),
            jax.ShapeDtypeStruct((length, 128), jnp.float32),
        ),
        in_specs=[pl.BlockSpec(memory_space=pltpu.SMEM), vmem, vmem, vmem],
        out_specs=(vmem, vmem, vmem),
        scratch_shapes=[
            pltpu.VMEM((length, width), jnp.bfloat16),
            pltpu.VMEM((length, width), jnp.bfloat16),
            pltpu.VMEM((head_count, length, 256), jnp.bfloat16),
        ],
        compiler_params=pltpu.CompilerParams(vmem_limit_bytes=60 << 20),
        name="attend_forward",
    )(spans, queries, key_rows, value_rows)


def backward_kernel(
    keys_of,
    rows_of,
    head_count,
    spans,
    q_ref,
    k_ref,
    v_ref,
    d_ref,
    mixed_rot_ref,
    log_ref,
    dq_ref,
    dk_ref,
    dv_ref,
    q_turned,
    d_turned,
    k_rot,
    v_rot,
    k_turned,
    q_heads,
    d_heads,
    dq_turned,
    dk_rot,
    dv_rot,
    log_rows,
    deltas,
):
    length, width = q_ref.shape
    small = length - LONGEST
    offset, border = spans[0], spans[1]
    low, full = jnp.bfloat16, jnp.float32

    def rotated(ref):
        return pltpu.roll(ref[...].astype(full), length - offset, 0)

    q_all = rotated(q_ref)
    q_turned[...] = jnp.transpose(q_all).astype(low)
    k_all = rotated(k_ref)
    k_rot[...] = k_all.astype(low)
    k_turned[...] = jnp.transpose(k_all).astype(low)
    v_rot[...] = rotated(v_ref).astype(low)
    d_all = rotated(d_ref)
    d_turned[...] = jnp.transpose(d_all).astype(low)
    for head in range(head_count):
        q_heads[head] = keep_head(head, q_all.astype(low))
        d_heads[head] = keep_head(head, d_all.astype(low))
    products = jnp.transpose(d_all * mixed_rot_ref[...])
    for head in range(head_count):
        deltas[head : head + 1, :] = jnp.sum(products[head * HEAD : (head + 1) * HEAD, :], axis=0, keepdims=True)
    log_rows[...] = jnp.transpose(log_ref[...])[0:8, :]
    dq_turned[...] = jnp.zeros_like(dq_turned)

    def block(key_row, row_base, row_count, masked):
        keys = pl.ds(key_row, keys_of)
        dk_sum = jnp.zeros((keys_of, width), full)
        dv_sum = jnp.zeros((keys_of, width), full)
        for head in range(head_count):
            k_head = keep_head(head, k_rot[keys, :])
            v_head = keep_head(head, v_rot[keys, :])
            lanes = slice(head * HEAD, (head + 1) * HEAD)
            k_side = k_turned[lanes, keys]
            for chunk in range(row_count // rows_of):
                start = row_base + chunk * rows_of
                rows = slice(start, start + rows_of)
                scores = dot(k_head, q_turned[:, rows], NN)
                dprobs = dot(v_head, d_turned[:, rows], NN)
                probs = jnp.exp2(scores * LOG_SCALE - log_rows[head : head + 1, rows])
                if masked:
                    shape = (keys_of, rows_of)
                    key_id = lax.broadcasted_iota(jnp.int32, shape, 0) + (key_row - LONGEST)
                    row_id = lax.broadcasted_iota(jnp.int32, shape, 1) + chunk * rows_of
                    probs = jnp.where((row_id < border) == (key_id < border), probs, 0.0)
                dv_sum = dv_sum + dot(probs.astype(low), d_heads[head, rows, :], NN)
                draw = (probs * (dprobs - deltas[head : head + 1, rows])).astype(low)
                dk_sum = dk_sum + dot(draw, q_heads[head, rows, :], NN)
                dq_turned[lanes, rows] += dot(k_side, draw, NN)
        dk_rot[keys, :] = dk_sum * SCALE
        dv_rot[keys, :] = dv_sum

    def large(index, nothing):
        block(pl.multiple_of(index * keys_of, keys_of), 0, LONGEST, False)
        return nothing

    def little(index, nothing):
        block(pl.multiple_of(LONGEST + index * keys_of, keys_of), LONGEST, small, True)
        return nothing

    lax.fori_loop(0, LONGEST // keys_of, large, 0)
    lax.fori_loop(0, small // keys_of, little, 0)
    dq_ref[...] = pltpu.roll(jnp.transpose(dq_turned[...] * SCALE), offset, 0).astype(low)
    dk_ref[...] = pltpu.roll(dk_rot[...], offset, 0).astype(low)
    dv_ref[...] = pltpu.roll(dv_rot[...], offset, 0).astype(low)


def attend_backward(spans, queries, key_rows, value_rows, grad_mixed, mixed_rot, log_totals):
    length, width = queries.shape
    head_count = width // HEAD
    vmem = pl.BlockSpec(memory_space=pltpu.VMEM)
    low, full = jnp.bfloat16, jnp.float32
    return pl.pallas_call(
        functools.partial(backward_kernel, 256, 512, head_count),
        out_shape=(jax.ShapeDtypeStruct((length, width), low),) * 3,
        in_specs=[pl.BlockSpec(memory_space=pltpu.SMEM)] + [vmem] * 6,
        out_specs=(vmem,) * 3,
        scratch_shapes=[
            pltpu.VMEM((width, length), low),
            pltpu.VMEM((width, length), low),
            pltpu.VMEM((length, width), low),
            pltpu.VMEM((length, width), low),
            pltpu.VMEM((width, length), low),
            pltpu.VMEM((head_count, length, width), low),
            pltpu.VMEM((head_count, length, width), low),
            pltpu.VMEM((width, length), full),
            pltpu.VMEM((length, width), full),
            pltpu.VMEM((length, width), full),
            pltpu.VMEM((8, length), full),
            pltpu.VMEM((8, length), full),
        ],
        compiler_params=pltpu.CompilerParams(vmem_limit_bytes=60 << 20),
        name="attend_backward",
    )(spans, queries, key_rows, value_rows, grad_mixed, mixed_rot, log_totals)


def local(
    layer_input,
    segment_ids,
    cotangent,
    attn_gain,
    attn_shift,
    query_weight,
    query_bias,
    key_weight,
    value_weight,
    value_bias,
    out_weight,
    out_bias,
    ffn_gain,
    ffn_shift,
    up_weight,
    up_bias,
    down_weight,
    down_bias,
):
    low_type = jnp.bfloat16
    spans = rotation(segment_ids[0], LONGEST)
    inputs = layer_input.astype(jnp.float32)
    normed_one, norm_one_back = jax.vjp(
        layer_norm, inputs, attn_gain.astype(jnp.float32), attn_shift.astype(jnp.float32)
    )
    normed_low = normed_one.astype(low_type)
    normed_rows = lax.all_gather(normed_low, "seq", axis=0, tiled=True)
    queries = (matmul(normed_rows, query_weight) + query_bias).astype(low_type)
    key_rows = matmul(normed_rows, key_weight).astype(low_type)
    value_rows = (matmul(normed_rows, value_weight) + value_bias).astype(low_type)
    mixed_low, mixed_rot, log_totals = attend_forward(spans, queries, key_rows, value_rows)
    middle = inputs + (
        lax.psum_scatter(matmul(mixed_low, out_weight), "seq", scatter_dimension=0, tiled=True)
        + out_bias
    )
    normed_two, norm_two_back = jax.vjp(
        layer_norm, middle, ffn_gain.astype(jnp.float32), ffn_shift.astype(jnp.float32)
    )
    normed_rows_two, cotangent_rows = (
        lax.all_gather(normed_two.astype(low_type), "seq", axis=0, tiled=True),
        lax.all_gather(cotangent, "seq", axis=0, tiled=True),
    )
    pre_act = matmul(normed_rows_two, up_weight) + up_bias
    hidden_float, gelu_back = jax.vjp(exact_gelu, pre_act)
    hidden_low = hidden_float.astype(low_type)
    layer_output = (
        middle
        + lax.psum_scatter(
            matmul(hidden_low, down_weight).astype(jnp.bfloat16),
            "seq",
            scatter_dimension=0,
            tiled=True,
        ).astype(jnp.float32)
        + down_bias
    ).astype(low_type)
    grad_output = cotangent.astype(jnp.float32)
    grad_down_weight = contract_rows(hidden_low, cotangent_rows)
    grad_down_bias = jnp.sum(grad_output, axis=0)
    grad_pre = gelu_back(outer_back(cotangent_rows, down_weight))[0].astype(low_type)
    grad_up_bias = jnp.sum(grad_pre.astype(jnp.float32), axis=0)
    grad_up_weight = contract_rows(normed_rows_two, grad_pre)
    grad_normed_two = lax.psum_scatter(
        outer_back(grad_pre, up_weight), "seq", scatter_dimension=0, tiled=True
    )
    grad_mid_part, grad_ffn_gain, grad_ffn_shift = norm_two_back(grad_normed_two)
    grad_middle = grad_output + grad_mid_part
    grad_branch = grad_middle.astype(low_type)
    grad_out_bias = jnp.sum(grad_branch.astype(jnp.float32), axis=0)
    branch_rows = lax.all_gather(grad_branch, "seq", axis=0, tiled=True)
    grad_out_weight = contract_rows(mixed_low, branch_rows)
    grad_mixed = outer_back(branch_rows, out_weight).astype(low_type)
    grad_q_low, grad_k_low, grad_v_low = attend_backward(
        spans, queries, key_rows, value_rows, grad_mixed, mixed_rot, log_totals
    )
    grad_query_weight = contract_rows(normed_rows, grad_q_low)
    grad_key_weight = contract_rows(normed_rows, grad_k_low)
    grad_value_weight = contract_rows(normed_rows, grad_v_low)
    grad_query_bias = jnp.sum(grad_q_low.astype(jnp.float32), axis=0)
    grad_value_bias = jnp.sum(grad_v_low.astype(jnp.float32), axis=0)
    part_q = outer_back(grad_q_low, query_weight)
    part_k = outer_back(grad_k_low, key_weight)
    part_v = outer_back(grad_v_low, value_weight)
    grad_normed_one = lax.psum_scatter(
        (part_q + part_k + part_v).astype(jnp.bfloat16), "seq", scatter_dimension=0, tiled=True
    ).astype(jnp.float32)
    grad_in_part, grad_attn_gain, grad_attn_shift = norm_one_back(grad_normed_one)
    input_grad = grad_middle + grad_in_part
    (
        grad_query_weight,
        grad_key_weight,
        grad_value_weight,
        grad_out_weight,
        grad_up_weight,
        grad_down_weight,
        grad_query_bias,
        grad_value_bias,
        grad_up_bias,
    ) = lax.psum(
        (
            grad_query_weight,
            grad_key_weight,
            grad_value_weight,
            grad_out_weight,
            grad_up_weight,
            grad_down_weight,
            grad_query_bias,
            grad_value_bias,
            grad_up_bias,
        ),
        "dp",
    )
    (
        grad_attn_gain,
        grad_attn_shift,
        grad_out_bias,
        grad_ffn_gain,
        grad_ffn_shift,
        grad_down_bias,
    ) = lax.psum(
        (
            grad_attn_gain,
            grad_attn_shift,
            grad_out_bias,
            grad_ffn_gain,
            grad_ffn_shift,
            grad_down_bias,
        ),
        ("dp", "seq"),
    )
    return (
        layer_output,
        input_grad,
        grad_attn_gain,
        grad_attn_shift,
        grad_query_weight,
        grad_query_bias,
        grad_key_weight,
        grad_value_weight,
        grad_value_bias,
        grad_out_weight,
        grad_out_bias,
        grad_ffn_gain,
        grad_ffn_shift,
        grad_up_weight,
        grad_up_bias,
        grad_down_weight,
        grad_down_bias,
    )


def solution(mesh):
    return jax.shard_map(
        local,
        mesh=mesh,
        in_specs=(
            P(("dp", "seq"), None),
            P("dp", None),
            P(("dp", "seq"), None),
            P(),
            P(),
            P(None, "seq"),
            P("seq"),
            P(None, "seq"),
            P(None, "seq"),
            P("seq"),
            P("seq", None),
            P(),
            P(),
            P(),
            P(None, "seq"),
            P("seq"),
            P("seq", None),
            P(),
        ),
        out_specs=(
            P(("dp", "seq"), None),
            P(("dp", "seq"), None),
            P(),
            P(),
            P(None, "seq"),
            P("seq"),
            P(None, "seq"),
            P(None, "seq"),
            P("seq"),
            P("seq", None),
            P(),
            P(),
            P(),
            P(None, "seq"),
            P("seq"),
            P("seq", None),
            P(),
        ),
        check_vma=False,
    )
```

time: 1380 us -> 813 us (0.59)
  matrix products: 321 us -> 88.2 us
  loops' own time: 170 us -> 0 us
  blocking collectives: 187 us -> 64.5 us
  Pallas kernels: 0 us -> 95 us
  waiting for transfers between devices: 552 us -> 469 us
  local copies, waits for them, and re-layouts: 58.6 us -> 20 us
  other arithmetic: 64.9 us -> 34.9 us
    dot_general x153 -> x0, matrix products: 234 us -> none  [the longest x34 74 us: tile_parts(): jnp.einsum('qhd,khd->hqk', grad_block, value_tile, preferred_element_type...]
    another operation x22 -> x0, loops' own time: 170 us -> none  [the longest x5 59.8 us: one_block(): lax.fori_loop(lower_tiles[block_index], upper_tiles[block_index], grad_pa...]
    psum x1, blocking collectives: 146 us -> 22.4 us  [local(): lax.psum((grad_query_weight, grad_key_weight, grad_value_weight, grad_out...]
    pallas_call x0 -> x2, Pallas kernels: none -> 95 us  [the longest x1 60.3 us: attend_backward(): pl.pallas_call(functools.partial(backward_kernel, 256, 512, head_count),...]
    reduce_scatter x1, waiting for transfers between devices: 133 us -> 68.5 us  [local(): lax.psum_scatter(matmul(mixed_low, out_weight), 'seq', scatter_dimension=...]
    dynamic_slice x118 -> x0, local copies, waits for them, and re-layouts: 30.8 us -> none  [the longest x10 5.89 us: one_block(): upper_tiles[block_index]]
    eq x68 -> x0, other arithmetic: 14.7 us -> none  [the longest x51 11 us: tile_probs(): same_doc = (seg_query[:, None] == seg_key[None, :])[None]]
  transfers between devices with their start and end apart: 9 -> 9, of which waited for: 8 -> 8; matrix products, arithmetic and copies ran while one was open for 4% -> 7% of each run, Pallas kernels for 0% -> 0%
where the time goes in v1:
time: 813 us; the launch traced here: 803 us
  waiting for transfers between devices  469 us (58%)
  Pallas kernels  95 us (12%)
  matrix products  88.2 us (11%)
  blocking collectives  64.5 us (8%)
  other arithmetic  34.9 us (4%)
  between operations  20.5 us (3%)
  local copies, waits for them, and re-layouts  20 us (2%)
  starting transfers between devices  10.9 us (1%)
    psum x1, waiting for transfers between devices, local(): lax.psum((grad_query_weight, grad_key_weight, grad_value_weight, grad_out...  193 us
    reduce_scatter x1, waiting for transfers between devices, local(): lax.psum_scatter(matmul(mixed_low, out_weight), 'seq', scatter_dimension=...  68.5 us
    pallas_call x1, Pallas kernels, attend_backward(): pl.pallas_call(functools.partial(backward_kernel, 256, 512, head_count),...  60.3 us
    reduce_scatter x1, waiting for transfers between devices, local(): lax.psum_scatter(outer_back(grad_pre, up_weight), 'seq', scatter_dimensio...  55.1 us
    reduce_scatter x1, waiting for transfers between devices, local(): lax.psum_scatter(matmul(hidden_low, down_weight).astype(jnp.bfloat16), 's...  43 us
    psum x1, blocking collectives, local(): lax.psum((grad_attn_gain, grad_attn_shift, grad_out_bias, grad_ffn_gain,...  42.1 us
    dot_general x6, matrix products, outer_back(): lax.dot_general(left_side, right_side, (((1,), (1,)), ((), ())), preferre...  39.5 us
    pallas_call x1, Pallas kernels, attend_forward(): pl.pallas_call(functools.partial(forward_kernel, 512, 512, head_count), o...  34.7 us
  transfers between devices with their start and end apart: 9, of which 8 were waited for; matrix products, arithmetic and copies ran while one was open for 7% of the time, Pallas kernels for 0%

profile of v1, /device:TPU:0, one launch (start us, length us, event | category | flops | bytes accessed | tf_op | source)
XLA Modules:
  0.0 803.3 jit_solution(2588609550697577987)
XLA Ops:
  13.0 2.6 fusion.15
  22.8 28.7 %all-gather.5.cloned.1.call-done = bf16[2560,768]{1,0:T(8,128)(2,1)} async-done(((bf16[640,768]{1,0:T(8,128)(2,1)}), bf16[2560,768]{1,0:T(8,128)(2,1)}) %all-gather.5.cloned.1.call-update) | async-done | bytes 3932176 | tf_op jit(solution)/shard_map/all_gather | solution.py:301
  51.5 4.5 convolution_convert_fusion.1.k_ref
  56.0 2.3 fusion.7.v_ref
  58.3 2.3 fusion.6.q_ref
  60.7 34.7 %attend_forward.1 = (bf16[2560,192]{1,0:T(8,128)(2,1)}, f32[2560,192]{1,0:T(8,128)}, f32[2560,128]{1,0:T(8,128)}) custom-call(s32[2]{0:T(128)} %pad_add_fusion.spans, bf16[2560,192]{1,0:T(8,128)(2,1)} %fusion.6.q_ref, bf16[2560,192]{1,0:T(8,128)(2,1)} %convolution_convert_fusion.1.k_ref, bf16[2560,192]{1,0:T(8,128)(2,1)} %fusion.7.v_ref), custom_call_target="tpu_custom_call" | custom-call | tf_op jit(solution)/shard_map/attend_forward/pallas_call | solution.py:132
  95.4 5.6 fusion.29
  101.6 68.5 %reduce-scatter.5.cloned.1.call-done = f32[640,768]{1,0:T(8,128)} async-done(((f32[2560,768]{1,0:T(8,128)}), f32[640,768]{1,0:T(8,128)}) %reduce-scatter.5.cloned.1.call-update) | async-done | bytes 1966096 | tf_op jit(solution)/shard_map/reduce_scatter | solution.py:307
  174.6 10.4 %reduce-scatter.9.cloned.1.call-start = ((), (), s32[]{:S(2)}) async-start(), calls=%async_computation.9 | async-start | bytes 9830400 | tf_op jit(solution)/shard_map/reduce_scatter | solution.py:336
  185.0 22.1 %all-gather.7.cloned.1.call-done = bf16[2560,768]{1,0:T(8,128)(2,1)} async-done(((bf16[640,768]{1,0:T(8,128)(2,1)}), bf16[2560,768]{1,0:T(8,128)(2,1)}) %all-gather.7.cloned.1.call-update) | async-done | bytes 3932176 | tf_op jit(solution)/shard_map/all_gather | solution.py:314
  207.1 8.9 %fusion.30 = f32[2560,768]{1,0:T(8,128)} fusion(bf16[2560,768]{1,0:T(8,128)(2,1)} %all-gather.7.cloned.1.call-done, bf16[768,768]{1,0:T(8,128)(2,1)} %param.32), kind=kOutput, calls=%fused_computation.76 | convolution fusion | flops 3019898880 | bytes 12976128 | tf_op jit(solution)/shard_map/dot_general | solution.py:33
  216.0 25.6 %all-gather.9.cloned.1.call-done = bf16[2560,768]{1,0:T(8,128)(2,1)} async-done(((bf16[640,768]{1,0:T(8,128)(2,1)}), bf16[2560,768]{1,0:T(8,128)(2,1)}) %all-gather.9.cloned.1.call-update) | async-done | bytes 3932176 | tf_op jit(solution)/shard_map/all_gather | solution.py:315
  241.6 23.8 %convert_reduce_fusion = (f32[768]{0:T(1024)S(1)}, bf16[2560,768]{1,0:T(8,128)(2,1)S(1)}, f32[2560,768]{1,0:T(8,128)}) fusion(f32[2560,768]{1,0:T(8,128)} %fusion.30, f32[768]{0:T(1024)S(1)} %convert_element_type.110, bf16[2560,768]{1,0:T(8,128)(2,1)} %all-gather.9.cloned.1.call-done, bf16[768,768]{1,0:T(8,128)(2,1)S(1)} %copy-done), kind=kOutput, calls=%fused_computation.2 | convolution fusion | flops 3167354112 | bytes 24778752 | tf_op jit(solution)/shard_map/dot_general | solution.py:43
  267.3 5.4 fusion.31
  272.7 6.7 multiply_convert_fusion
  281.3 4.7 convolution_convert_fusion
  286.7 55.1 %reduce-scatter.9.cloned.1.call-done = f32[640,768]{1,0:T(8,128)} async-done(((f32[2560,768]{1,0:T(8,128)}), f32[640,768]{1,0:T(8,128)}) %reduce-scatter.9.cloned.1.call-update) | async-done | bytes 1966096 | tf_op jit(solution)/shard_map/reduce_scatter | solution.py:336
  341.8 2.3 multiply_reduce_fusion
  344.1 43.0 %reduce-scatter.7.cloned.1.call-done = bf16[640,768]{1,0:T(8,128)(2,1)} async-done(((bf16[2560,768]{1,0:T(8,128)(2,1)}), bf16[640,768]{1,0:T(8,128)(2,1)}) %reduce-scatter.7.cloned.1.call-update) | async-done | bytes 983056 | tf_op jit(solution)/shard_map/reduce_scatter | solution.py:322
  387.1 3.7 fusion.27
  393.4 33.1 %all-gather.11.cloned.1.call-done = bf16[2560,768]{1,0:T(8,128)(2,1)} async-done(((bf16[640,768]{1,0:T(8,128)(2,1)}), bf16[2560,768]{1,0:T(8,128)(2,1)}) %all-gather.11.cloned.1.call-update) | async-done | bytes 3932176 | tf_op jit(solution)/shard_map/all_gather | solution.py:343
  426.6 3.5 convolution_convert_fusion.2
  431.7 60.3 %attend_backward.1 = (bf16[2560,192]{1,0:T(8,128)(2,1)}, bf16[2560,192]{1,0:T(8,128)(2,1)}, bf16[2560,192]{1,0:T(8,128)(2,1)}) custom-call(s32[2]{0:T(128)} %pad_add_fusion.spans, bf16[2560,192]{1,0:T(8,128)(2,1)} %fusion.6.q_ref, bf16[2560,192]{1,0:T(8,128)(2,1)} %convolution_convert_fusion.1.k_ref, bf16[2560,192]{1,0:T(8,128)(2,1)} %fusion.7.v_ref, ...), custom_call_target="tpu_custom_call" | custom-call | tf_op jit(solution)/shard_map/attend_backward/pallas_call | solution.py:250
  492.0 2.6 fusion.32
  496.0 3.0 add_convert_fusion
  499.4 8.2 %fusion.38 = f32[768,768]{1,0:T(8,128)} fusion(bf16[2560,768]{1,0:T(8,128)(2,1)} %all-gather.7.cloned.1.call-done, bf16[2560,768]{1,0:T(8,128)(2,1)} %copy-done.45), kind=kOutput, calls=%fused_computation.84 | convolution fusion | flops 3019898880 | bytes 10223616 | tf_op jit(solution)/shard_map/dot_general | solution.py:37
  507.6 4.8 fusion.39
  520.8 2.3 convert_reduce_fusion.3
  523.1 22.4 %all-reduce.1 = (f32[192]{0:T(256)}, f32[192]{0:T(256)}, f32[768]{0:T(1024)}) all-reduce(f32[192]{0:T(256)S(1)} %get-tuple-element.66, f32[192]{0:T(256)S(1)} %get-tuple-element.65, f32[768]{0:T(1024)S(1)} %get-tuple-element.53), channel_id=1, replica_groups=mesh['dp'=8,'seq'=4] {'dp'}, use_global_device_ids=true, to_apply=%region_20.21 | all-reduce | flops 1152 | bytes 9216 | tf_op jit(solution)/shard_map/psum | solution.py:372
  547.5 2.3 fusion.18
  552.0 42.1 %all-reduce = (f32[768]{0:T(1024)}, f32[768]{0:T(1024)}, f32[768]{0:T(1024)}, f32[768]{0:T(1024)}, f32[768]{0:T(1024)}, /*index=5*/f32[768]{0:T(1024)}) all-reduce(f32[768]{0:T(1024)S(1)} %get-tuple-element.31, f32[768]{0:T(1024)S(1)} %get-tuple-element.34, ...), channel_id=1, replica_groups=mesh['dp'=8,'seq'=4] {'dp','seq'}, use_global_device_ids=true, to_apply=%region_15.16 | all-reduce | flops 4608 | bytes 36864 | tf_op jit(solution)/shard_map/psum | solution.py:393
  594.2 192.5 %all-reduce.5.cloned.1.call-done = (f32[768,192]{0,1:T(8,128)}, f32[768,192]{0,1:T(8,128)}, f32[768,192]{0,1:T(8,128)}, f32[192,768]{1,0:T(8,128)}, f32[768,768]{1,0:T(8,128)}, /*index=5*/f32[768,768]{1,0:T(8,128)}) async-done(((f32[768,192]{0,1:T(8,128)}, f32[768,192]{0,1:T(8,128)}, f32[768,192]{0,1:T(8,128)}, f32[192,768]{1,0:T(8,128)}, f32[768,768]{1,0:T(8,128)}, /*index=5*/f32[768,768]{1,0:T(8,128)}), ...) | async-done | bytes 7077904 | tf_op jit(solution)/shard_map/psum | solution.py:372
  (149 shorter events, 44.8 us)
Async XLA Ops:
  7.2 234.5 %copy-start = (bf16[768,768]{1,0:T(8,128)(2,1)S(1)}, bf16[768,768]{1,0:T(8,128)(2,1)}, u32[]{:S(2)}) copy-start(bf16[768,768]{1,0:T(8,128)(2,1)} %param.34) | copy-start | bytes 3538948
  7.2 8.4 %copy-start.32 = (s32[1,2560]{1,0:T(1,128)S(1)}, s32[1,2560]{1,0:T(1,128)}, u32[]{:S(2)}) copy-start(s32[1,2560]{1,0:T(1,128)} %param.19) | copy-start | bytes 30724
  7.2 11.7 %copy-start.43 = (bf16[192]{0:T(256)(128)(2,1)S(1)}, bf16[192]{0:T(256)(128)(2,1)}, u32[]{:S(2)}) copy-start(bf16[192]{0:T(256)(128)(2,1)} %param.24) | copy-start | bytes 1156
  7.2 11.7 %copy-start.44 = (bf16[192]{0:T(256)(128)(2,1)S(1)}, bf16[192]{0:T(256)(128)(2,1)}, u32[]{:S(2)}) copy-start(bf16[192]{0:T(256)(128)(2,1)} %param.27) | copy-start | bytes 1156
  7.2 44.2 %copy-start.20 = (bf16[768,192]{0,1:T(8,128)(2,1)S(1)}, bf16[768,192]{0,1:T(8,128)(2,1)}, u32[]{:S(2)}) copy-start(bf16[768,192]{0,1:T(8,128)(2,1)} %param.25) | copy-start | bytes 884740
  7.2 44.2 %all-gather.5.cloned.1.call-start = ((), (), s32[]{:S(2)}) async-start(), calls=%async_computation.4 | async-start | bytes 4915200 | tf_op jit(solution)/shard_map/all_gather | solution.py:301
  15.6 154.5 %reduce-scatter.5.cloned.1.call-start = ((), (), s32[]{:S(2)}) async-start(), calls=%async_computation.5 | async-start | bytes 9830400 | tf_op jit(solution)/shard_map/reduce_scatter | solution.py:307
  22.8 33.2 %copy-start.22 = (bf16[768,192]{0,1:T(8,128)(2,1)S(1)}, bf16[768,192]{0,1:T(8,128)(2,1)}, u32[]{:S(2)}) copy-start(bf16[768,192]{0,1:T(8,128)(2,1)} %param.26) | copy-start | bytes 884740
  60.7 34.7 %copy-start.17 = (bf16[192,768]{1,0:T(8,128)(2,1)S(1)}, bf16[192,768]{1,0:T(8,128)(2,1)}, u32[]{:S(2)}) copy-start(bf16[192,768]{1,0:T(8,128)(2,1)} %param.28) | copy-start | bytes 884740
  100.9 106.2 %all-gather.7.cloned.1.call-start = ((), (), s32[]{:S(2)}) async-start(), calls=%async_computation.6 | async-start | bytes 4915200 | tf_op jit(solution)/shard_map/all_gather | solution.py:314
  172.3 12.7 %copy-start.36 = (bf16[768]{0:T(1024)(128)(2,1)S(1)}, bf16[768]{0:T(1024)(128)(2,1)}, u32[]{:S(2)}) copy-start(bf16[768]{0:T(1024)(128)(2,1)} %param.33) | copy-start | bytes 4612
  174.0 67.7 %all-gather.9.cloned.1.call-start = ((), (), s32[]{:S(2)}) async-start(), calls=%async_computation.8 | async-start | bytes 4915200 | tf_op jit(solution)/shard_map/all_gather | solution.py:315
  174.6 167.2 %reduce-scatter.9.cloned.1.call-start = ((), (), s32[]{:S(2)}) async-start(), calls=%async_computation.9 | async-start | bytes 9830400 | tf_op jit(solution)/shard_map/reduce_scatter | solution.py:336
  241.6 25.6 %copy-start.42 = (bf16[768,768]{1,0:T(8,128)(2,1)S(1)}, bf16[768,768]{1,0:T(8,128)(2,1)}, u32[]{:S(2)}) copy-start(bf16[768,768]{1,0:T(8,128)(2,1)} %param.32) | copy-start | bytes 3538948
  272.7 114.5 %reduce-scatter.7.cloned.1.call-start = ((), (), s32[]{:S(2)}) async-start(), calls=%async_computation.7 | async-start | bytes 4915200 | tf_op jit(solution)/shard_map/reduce_scatter | solution.py:322
  286.0 140.5 %all-gather.11.cloned.1.call-start = ((), (), s32[]{:S(2)}) async-start(), calls=%async_computation.10 | async-start | bytes 4915200 | tf_op jit(solution)/shard_map/all_gather | solution.py:343
  387.1 5.0 copy-start.5
  393.4 152.0 %reduce-scatter.11.cloned.1.call-start = ((), (), s32[]{:S(2)}) async-start(), calls=%async_computation.11 | async-start | bytes 4915200 | tf_op jit(solution)/shard_map/reduce_scatter | solution.py:357
  431.7 60.3 %copy-start.19 = (bf16[768,192]{0,1:T(8,128)(2,1)S(1)}, bf16[768,192]{0,1:T(8,128)(2,1)}, u32[]{:S(2)}) copy-start(bf16[768,192]{0,1:T(8,128)(2,1)} %param.23) | copy-start | bytes 884740
  499.1 287.6 %all-reduce.5.cloned.1.call-start = ((), (), s32[]{:S(2)}) async-start(), calls=%async_computation.12 | async-start | bytes 14155776 | tf_op jit(solution)/shard_map/psum | solution.py:372
  499.4 8.2 %copy-start.10 = (bf16[2560,768]{1,0:T(8,128)(2,1)S(1)}, bf16[2560,768]{1,0:T(8,128)(2,1)}, u32[]{:S(2)}) copy-start(bf16[2560,768]{1,0:T(8,128)(2,1)} %copy-done.9) | copy-start | bytes 11796484
  499.4 8.2 %copy-start.40 = (bf16[2560,768]{1,0:T(8,128)(2,1)S(1)}, bf16[2560,768]{1,0:T(8,128)(2,1)}, u32[]{:S(2)}) copy-start(bf16[2560,768]{1,0:T(8,128)(2,1)} %all-gather.9.cloned.1.call-done) | copy-start | bytes 11796484
  507.6 4.9 copy-start.11
  520.7 24.8 %copy-start.1 = (bf16[640,768]{1,0:T(8,128)(2,1)S(1)}, bf16[640,768]{1,0:T(8,128)(2,1)}, u32[]{:S(2)}) copy-start(bf16[640,768]{1,0:T(8,128)(2,1)} %param.18) | copy-start | bytes 2949124
  520.7 24.8 %copy-start.25 = (f32[640]{0:T(1024)S(1)}, f32[640]{0:T(1024)}, u32[]{:S(2)}) copy-start(f32[640]{0:T(1024)} %copy-done.24) | copy-start | bytes 7684
  520.7 24.8 %copy-start.27 = (f32[768]{0:T(1024)S(1)}, f32[768]{0:T(1024)}, u32[]{:S(2)}) copy-start(f32[768]{0:T(1024)} %copy-done.26) | copy-start | bytes 9220
  520.7 26.8 %copy-start.31 = (f32[640]{0:T(1024)S(1)}, f32[640]{0:T(1024)}, u32[]{:S(2)}) copy-start(f32[640]{0:T(1024)} %copy-done.30) | copy-start | bytes 7684
  520.7 26.8 %copy-start.29 = (f32[640]{0:T(1024)S(1)}, f32[640]{0:T(1024)}, u32[]{:S(2)}) copy-start(f32[640]{0:T(1024)} %copy-done.28) | copy-start | bytes 7684
  520.7 29.2 %copy-start.6 = (bf16[640,768]{1,0:T(8,128)(2,1)S(1)}, bf16[640,768]{1,0:T(8,128)(2,1)}, u32[]{:S(2)}) copy-start(bf16[640,768]{1,0:T(8,128)(2,1)} %param.20) | copy-start | bytes 2949124
  786.7 6.1 copy-start.16
  786.7 6.9 copy-start.15
  788.8 6.2 copy-start.14
  (23 other events, 50.6 us)
Sparse Core Ops, SparseCore 0:
  15.7 35.6 all-gather.4
  101.1 69.0 reduce-scatter.4
  174.1 32.9 all-gather.6
  208.6 32.9 all-gather.8
  272.8 68.9 reduce-scatter.8
  344.2 42.8 reduce-scatter.6
  393.5 32.9 all-gather.10
  499.2 42.8 reduce-scatter.10
  548.4 238.2 all-reduce.4
